TPU v7x, 32 devices: a whole 2x2x4 slice. The times are simulated.
32 devices in a mesh: row: 4 (over y, x), col: 4 (over z), layer: 2 (over core).
Axes of the slice: x: 2, y: 2, z: 4, core: 2. Of those that a mesh axis runs over, the one named last changes fastest.
Arguments:
- occupancy: int32 [4, 512], P(None, ('col', 'layer')), may hold values from 0 to 1, as said below
- tiles: bfloat16 [8, 4, 64, 256, 256], P(('col', 'layer'), 'row'), may hold values from -0.0234375 to 0.0234375
- panel: float32 [131072, 2048], P(('col', 'layer'), 'row'), may hold values from -6 to 6
Outputs:
- product: float32 [1024, 2048], P(('col', 'layer'), 'row')
Inputs may be any that keep to these rules, and one draw needn't show every extreme that they name: `occupancy`: in every draw one whole column block is occupied, so that the stored tiles of one device fill all 64 slots.
All inputs are finite; a program needn't handle non-finite values.
Results may differ from a plain program's by a relative error of at most 0.0029.
Values may be sent and summed in bfloat16 or wider, within the bound.
No kernel may reach another device: no remote copies, remote signals or barrier semaphores. Data moves between devices by JAX's collectives and lax.ppermute only.
A program may use at most 192 MiB of HBM per device.

v0:
```python
import jax
import jax.numpy as jnp
from jax import lax
from jax.sharding import PartitionSpec as P


def positions(occ_block):
    flat = occ_block.reshape(-1)
    count = flat.shape[0]
    rank = jnp.cumsum(flat) - 1
    index = jnp.arange(count, dtype=jnp.int32)
    match = (flat[None, :] == 1) & (rank[None, :] == index[:, None])
    where_at = jnp.sum(jnp.where(match, index[None, :], 0), axis=1)
    valid = jnp.sum(match.astype(jnp.int32), axis=1)
    width = occ_block.shape[1]
    return (where_at // width, where_at % width, valid)


def local(occupancy, tiles, panel):
    tile_rows = occupancy.shape[0]
    width = occupancy.shape[1]
    side = tiles.shape[-1]
    slot_count = tiles.shape[2]
    columns = panel.shape[1]
    panel_low = panel.astype(jnp.bfloat16).reshape(width, side, columns)
    rows_at, cols_at, valid = positions(occupancy)
    target_rows = jnp.where(valid == 1, rows_at, tile_rows)
    empty = jnp.zeros((tile_rows, width, side, side), jnp.bfloat16)
    whole = lax.all_gather(tiles, "row", axis=1, tiled=True)
    count = whole.shape[1] * slot_count
    flat = whole.reshape(count, side, side)
    dense = empty.at[target_rows, cols_at].set(flat, mode="drop")
    partial_value = jnp.einsum(
        "itab,tbn->ian", dense, panel_low, preferred_element_type=jnp.float32
    )
    partial_value = partial_value.reshape(tile_rows * side, columns)
    product = lax.psum_scatter(partial_value, ("col", "layer"), scatter_dimension=0, tiled=True)
    return product


def solution(mesh):
    placed = (
        P(None, ("col", "layer")),
        P(("col", "layer"), "row", None, None, None),
        P(("col", "layer"), "row"),
    )
    return jax.shard_map(
        local, mesh=mesh, in_specs=placed, out_specs=P(("col", "layer"), "row"), check_vma=False
    )
```

profile of v0, /device:TPU:0, one launch (start us, length us, event | category | flops | bytes accessed | tf_op | source)
XLA Modules:
  0.0 538.8 jit_solution(5105429763188635338)
XLA Ops:
  6.5 0.0 all-gather.2.cloned.1.call-start
  6.5 0.7 all-gather.2.cloned.1.call-update
  7.3 0.0 reduce-scatter.2.cloned.1.call-start
  7.3 0.8 reshape.147
  8.1 0.3 reduce-window.9
  8.4 0.1 slice.7
  8.5 0.7 broadcast_compare_fusion
  9.2 0.1 eq.44
  9.3 21.7 %convert_element_type.7 = bf16[16384,512]{1,0:T(8,128)(2,1)} convert(f32[16384,512]{1,0:T(8,128)} %param.5) | non-fusion elementwise | flops 8388608 | bytes 50331648 | tf_op jit(solution)/shard_map/convert_element_type | solution.py:25
  30.9 0.1 slice_reduce_fusion
  31.1 0.1 add_bitcast_fusion
  31.1 0.2 select_reduce_fusion
  31.3 277.7 %all-gather.2.cloned.1.call-done = bf16[1,4,64,256,256]{4,3,2,0,1:T(8,128)(2,1)} async-done(((bf16[1,1,64,256,256]{4,3,2,0,1:T(8,128)(2,1)}), bf16[1,4,64,256,256]{4,3,2,0,1:T(8,128)(2,1)}) %all-gather.2.cloned.1.call-update) | async-done | bytes 33554448 | tf_op jit(solution)/shard_map/all_gather | solution.py:29
  309.0 10.9 %broadcast_in_dim.24 = bf16[4,64,256,256]{3,2,1,0:T(8,128)(2,1)} broadcast(bf16[]{:T(256)} %constant.34.clone.1), dimensions={} | broadcast | bytes 33554432 | tf_op jit(solution)/shard_map/broadcast_in_dim | solution.py:28
  319.9 68.2 %scatter_fusion = bf16[4,64,256,256]{3,2,1,0:T(8,128)(2,1)} fusion(bf16[4,64,256,256]{3,2,1,0:T(8,128)(2,1)} %broadcast_in_dim.24, s32[256]{0:T(256)S(1)} %bitcast.15, bf16[256,256,256]{2,1,0:T(8,128)(2,1)} %bitcast.13), kind=kCustom, calls=%fused_computation | custom fusion | bytes 100665344 | tf_op jit(solution)/shard_map/scatter | solution.py:32
  388.1 31.2 %copy.10 = bf16[4,256,256,64]{2,3,1,0:T(8,128)(2,1)} copy(bf16[4,256,256,64]{2,1,3,0:T(8,128)(2,1)} %bitcast.12) | data formatting | bytes 67108864 | tf_op jit(solution)/shard_map/itab,tbn->ian/dot_general | solution.py:33
  419.3 58.7 %fusion.2 = f32[1024,512]{1,0:T(8,128)} fusion(bf16[64,256,512]{2,1,0:T(8,128)(2,1)} %bitcast.16, bf16[1024,256,64]{1,2,0:T(8,128)(2,1)} %bitcast.14), kind=kOutput, calls=%fused_computation.3 | convolution fusion | flops 17179869184 | bytes 52428800 | tf_op jit(solution)/shard_map/itab,tbn->ian/dot_general | solution.py:33
  478.0 0.0 reduce-scatter.2.cloned.1.call-update
  478.0 53.9 %reduce-scatter.2.cloned.1.call-done = f32[128,512]{1,0:T(8,128)} async-done(((f32[1024,512]{1,0:T(8,128)}), f32[128,512]{1,0:T(8,128)}) %reduce-scatter.2.cloned.1.call-update) | async-done | bytes 262160 | tf_op jit(solution)/shard_map/reduce_scatter | solution.py:37
  (3 shorter events, 0.1 us)
Async XLA Ops:
  6.5 302.5 %all-gather.2.cloned.1.call-start = ((), (), s32[]{:S(2)}) async-start(), calls=%async_computation.1 | async-start | bytes 41943040 | tf_op jit(solution)/shard_map/all_gather | solution.py:29
  7.3 524.7 %reduce-scatter.2.cloned.1.call-start = ((), (), s32[]{:S(2)}) async-start(), calls=%async_computation.2 | async-start | bytes 2359296 | tf_op jit(solution)/shard_map/reduce_scatter | solution.py:37
Sparse Core Ops, SparseCore 0:
  9.2 299.7 all-gather.1
  478.2 53.7 reduce-scatter.1
where the time goes:
time: 540 us; the launch traced here: 539 us
  waiting for transfers between devices  332 us (61%)
  local copies, waits for them, and re-layouts  111 us (21%)
  matrix products  58.7 us (11%)
  other arithmetic  23 us (4%)
  between operations  13.4 us (2%)
    all_gather x1, waiting for transfers between devices, local(): whole = lax.all_gather(tiles, 'row', axis=1, tiled=True)  278 us
    scatter x1, local copies, waits for them, and re-layouts, local(): dense = empty.at[target_rows, cols_at].set(flat, mode='drop')  68.2 us
    dot_general x1, matrix products, local(): jnp.einsum('itab,tbn->ian', dense, panel_low, preferred_element_type=jnp....  58.7 us
    reduce_scatter x1, waiting for transfers between devices, local(): lax.psum_scatter(partial_value, ('col', 'layer'), scatter_dimension=0, ti...  53.9 us
    dot_general x1, local copies, waits for them, and re-layouts, local(): jnp.einsum('itab,tbn->ian', dense, panel_low, preferred_element_type=jnp....  31.2 us
    convert_element_type x1, other arithmetic, local(): panel_low = panel.astype(jnp.bfloat16).reshape(width, side, columns)  21.7 us
    broadcast_in_dim x1, local copies, waits for them, and re-layouts, local(): empty = jnp.zeros((tile_rows, width, side, side), jnp.bfloat16)  10.9 us
  transfers between devices with their start and end apart: 2, of which 2 were waited for; matrix products, arithmetic and copies ran while one was open for 4% of the time, Pallas kernels for 0%

commit v1 on v0

v1 whole, which is shorter than its diff:
```python
import functools

import jax
import jax.numpy as jnp
from jax import lax
from jax.experimental import pallas as pl
from jax.experimental.pallas import tpu as pltpu
from jax.sharding import PartitionSpec as P

LATENCY = 2
ANY = pl.BlockSpec(memory_space=pl.ANY)
SMEM = pl.BlockSpec(memory_space=pltpu.SMEM)


def ring_order(n_row):
    side = int(round(n_row ** 0.5))
    if side * side != n_row or side % 2:
        return list(range(n_row))
    path = [(0, x) for x in range(side)]
    for x in reversed(range(side)):
        ys = range(1, side) if (side - 1 - x) % 2 == 0 else reversed(range(1, side))
        path += [(y, x) for y in ys]
    return [y * side + x for y, x in path]


def plan_kernel(order, slots, chunk, steps, me_ref, occ_ref, where_ref, sched_ref, meta_ref, start_ref, quota_ref, owner_ref, held_ref):
    tile_rows, width = occ_ref.shape
    n = len(order)
    pair = 2 * chunk

    def mark(e, rank):
        where_ref[rank] = e
        return rank + occ_ref[e // width, e % width]

    count = lax.fori_loop(0, tile_rows * width, mark, jnp.int32(0))
    for p in range(n):
        stored = jnp.clip(count - slots * order[p], 0, slots)
        owner_ref[p] = order[p]
        held_ref[p] = stored
        quota_ref[p] = (stored + pair - 1) // pair

    def clear(t, carry):
        for f in range(8):
            sched_ref[t, f] = 0
        return carry

    lax.fori_loop(0, steps, clear, 0)
    total = jnp.int32(0)
    me = me_ref[0]
    for d in range(2):
        back = n - 1 if d == 0 else 1

        def first(p, carry):
            start_ref[0, p] = 0
            return jnp.maximum(carry, quota_ref[p])

        total = lax.fori_loop(0, n, first, total)

        def hop(h, carry):
            def place(p, c):
                up = (p + back) % n
                source = (p + h * back) % n
                last = (p + (h - 1) * back) % n
                begin = jnp.maximum(start_ref[h - 1, p] + quota_ref[last], start_ref[h - 1, up] + LATENCY)
                start_ref[h, p] = begin
                amount = quota_ref[source]
                return jnp.where(amount > 0, jnp.maximum(c, begin + amount), c)

            return lax.fori_loop(0, n, place, carry)

        total = lax.fori_loop(1, n - 1, hop, total)

        def fill(h, carry):
            up = (me + back) % n
            source = (me + h * back) % n
            begin = start_ref[h, me]
            arrived = start_ref[jnp.maximum(h - 1, 0), up]

            def send(q, c):
                sched_ref[begin + q, d] = jnp.where(h == 0, 2 * q + d, -1 - (arrived + q))
                return c

            lax.fori_loop(0, quota_ref[source], send, 0)
            origin = (up + h * back) % n
            begin_up = start_ref[h, up]

            def receive(q, c):
                slot = (2 * q + d) * chunk
                sched_ref[begin_up + q, 2 + 2 * d] = owner_ref[origin] * slots + slot
                sched_ref[begin_up + q, 3 + 2 * d] = jnp.clip(held_ref[origin] - slot, 0, chunk)
                return c

            lax.fori_loop(0, quota_ref[origin], receive, 0)
            return carry

        lax.fori_loop(0, n - 1, fill, 0)
    meta_ref[0] = total
    meta_ref[1] = held_ref[me]
    meta_ref[2] = owner_ref[me] * slots


def plan(occupancy, order, slots, chunk, steps):
    n = len(order)
    place = [0] * n
    for p, r in enumerate(order):
        place[r] = p
    me = jnp.asarray(place, jnp.int32)[lax.axis_index("row")].reshape(1)
    size = occupancy.shape[0] * occupancy.shape[1]
    return pl.pallas_call(
        functools.partial(plan_kernel, order, slots, chunk, steps),
        out_shape=(
            jax.ShapeDtypeStruct((size,), jnp.int32),
            jax.ShapeDtypeStruct((steps, 8), jnp.int32),
            jax.ShapeDtypeStruct((4,), jnp.int32),
        ),
        in_specs=[SMEM, SMEM],
        out_specs=(SMEM, SMEM, SMEM),
        scratch_shapes=[
            pltpu.SMEM((n, n), jnp.int32),
            pltpu.SMEM((n,), jnp.int32),
            pltpu.SMEM((n,), jnp.int32),
            pltpu.SMEM((n,), jnp.int32),
        ],
        name="plan",
    )(me, occupancy)


def accumulate(acc_ref, code, width, tile, panel_block):
    side = tile.shape[0]
    row = pl.multiple_of((code // width) * side, side)
    acc_ref[pl.ds(row, side), :] += jnp.dot(
        tile, panel_block.astype(jnp.bfloat16), preferred_element_type=jnp.float32
    )


def own_kernel(depth, where_ref, meta_ref, tiles_ref, panel_ref, acc_ref, tbuf, pbuf, tsem, psem):
    width = panel_ref.shape[0]
    held, base = meta_ref[1], meta_ref[2]
    acc_ref[...] = jnp.zeros_like(acc_ref)

    def copies(e):
        s = e % depth
        code = where_ref[base + e]
        return (
            pltpu.make_async_copy(tiles_ref.at[e], tbuf.at[s], tsem.at[s]),
            pltpu.make_async_copy(panel_ref.at[code % width], pbuf.at[s], psem.at[s]),
        )

    def begin(e):
        for c in copies(e):
            c.start()

    def warm(e, carry):
        begin(e)
        return carry

    lax.fori_loop(0, jnp.minimum(held, depth - 1), warm, 0)

    def body(e, carry):
        @pl.when(e + depth - 1 < held)
        def _():
            begin(e + depth - 1)

        for c in copies(e):
            c.wait()
        s = e % depth
        accumulate(acc_ref, where_ref[base + e], width, tbuf[s], pbuf[s])
        return carry

    lax.fori_loop(0, held, body, 0)


def own_product(where, meta, tiles, panel, tile_rows):
    slots, side, _ = tiles.shape
    columns = panel.shape[2]
    depth = 8
    return pl.pallas_call(
        functools.partial(own_kernel, depth),
        out_shape=jax.ShapeDtypeStruct((tile_rows * side, columns), jnp.float32),
        in_specs=[SMEM, SMEM, ANY, ANY],
        out_specs=pl.BlockSpec((tile_rows * side, columns), lambda: (0, 0)),
        scratch_shapes=[
            pltpu.VMEM((depth, side, side), jnp.bfloat16),
            pltpu.VMEM((depth, side, columns), jnp.float32),
            pltpu.SemaphoreType.DMA((depth,)),
            pltpu.SemaphoreType.DMA((depth,)),
        ],
        compiler_params=pltpu.CompilerParams(vmem_limit_bytes=32 << 20),
        cost_estimate=pl.CostEstimate(flops=2 * slots * side * side * columns, bytes_accessed=slots * side * (2 * side + 4 * columns), transcendentals=0),
        name="own",
    )(where, meta, tiles, panel)


def step_kernel(chunk, relay, where_ref, sched_ref, t_ref, ra_ref, rb_ref, tiles_ref, panel_ref, acc_in, log_in, acc_ref, *rest):
    if relay:
        log_ref, sa_ref, sb_ref, rbuf, pbuf, rsem, psem, lsem, ssem = rest
    else:
        rbuf, pbuf, rsem, psem = rest
    width = panel_ref.shape[0]
    t = t_ref[0]
    got = (ra_ref, rb_ref)
    base = [sched_ref[t - 1, 2 + 2 * d] for d in range(2)]
    count = [sched_ref[t - 1, 3 + 2 * d] for d in range(2)]
    fetch = [pltpu.make_async_copy(got[d], rbuf.at[d], rsem.at[d]) for d in range(2)]
    for d in range(2):
        fetch[d].start()

    def panel_copy(d, e):
        code = where_ref[base[d] + e]
        return pltpu.make_async_copy(panel_ref.at[code % width], pbuf.at[d, e], psem.at[d, e])

    for d in range(2):
        def begin(e, carry):
            panel_copy(d, e).start()
            return carry

        lax.fori_loop(0, count[d], begin, 0)
    if relay:
        out = (sa_ref, sb_ref)
        for d in range(2):
            item = sched_ref[t + 1, d]
            logged = -1 - item

            @pl.when(item >= 0)
            def _():
                first = pl.multiple_of(item * chunk, chunk)
                pltpu.make_async_copy(tiles_ref.at[pl.ds(first, chunk)], out[d], ssem.at[d]).start()

            @pl.when((item < 0) & (logged == t - 1))
            def _():
                pltpu.make_async_copy(got[d], out[d], ssem.at[d]).start()

            @pl.when((item < 0) & (logged != t - 1))
            def _():
                pltpu.make_async_copy(log_in.at[d, logged], out[d], ssem.at[d]).start()

    for d in range(2):
        fetch[d].wait()
        if relay:
            pltpu.make_async_copy(rbuf.at[d], log_ref.at[d, t - 1], lsem.at[d]).start()
    acc_ref[...] = acc_in[...]
    for d in range(2):
        def body(e, carry):
            panel_copy(d, e).wait()
            accumulate(acc_ref, where_ref[base[d] + e], width, rbuf[d, e], pbuf[d, e])
            return carry

        lax.fori_loop(0, count[d], body, 0)
    if relay:
        for d in range(2):
            pltpu.make_async_copy(rbuf.at[d], log_ref.at[d, t - 1], lsem.at[d]).wait()
            pltpu.make_async_copy(tiles_ref.at[pl.ds(0, chunk)], out[d], ssem.at[d]).wait()


def step(where, sched, t, ra, rb, tiles, panel, acc, log, relay=True):
    chunk, side, _ = ra.shape
    columns = panel.shape[2]
    acc_spec = pl.BlockSpec(acc.shape, lambda: (0, 0))
    send = jax.ShapeDtypeStruct(ra.shape, ra.dtype)
    send_spec = pl.BlockSpec(ra.shape, lambda: (0, 0, 0))
    out_shape = [jax.ShapeDtypeStruct(acc.shape, acc.dtype)]
    out_specs = [acc_spec]
    scratch = [
        pltpu.VMEM((2,) + ra.shape, ra.dtype),
        pltpu.VMEM((2, chunk, side, columns), jnp.float32),
        pltpu.SemaphoreType.DMA((2,)),
        pltpu.SemaphoreType.DMA((2, chunk)),
    ]
    aliases = {7: 0}
    if relay:
        out_shape += [jax.ShapeDtypeStruct(log.shape, log.dtype), send, send]
        out_specs += [ANY, send_spec, send_spec]
        scratch += [pltpu.SemaphoreType.DMA((2,)), pltpu.SemaphoreType.DMA((2,))]
        aliases[8] = 1
    return pl.pallas_call(
        functools.partial(step_kernel, chunk, relay),
        out_shape=out_shape,
        in_specs=[SMEM, SMEM, SMEM, ANY, ANY, ANY, ANY, acc_spec, ANY],
        out_specs=out_specs,
        scratch_shapes=scratch,
        input_output_aliases=aliases,
        compiler_params=pltpu.CompilerParams(vmem_limit_bytes=48 << 20),
        cost_estimate=pl.CostEstimate(flops=4 * chunk * side * side * columns, bytes_accessed=2 * chunk * side * (4 * side + 4 * columns), transcendentals=0),
        name="step" if relay else "last",
    )(where, sched, t.reshape(1), ra, rb, tiles, panel, acc, log)


def blank(shape, dtype):
    return pl.pallas_call(lambda out: None, out_shape=jax.ShapeDtypeStruct(shape, dtype), out_specs=ANY, name="blank")()


def scatter_sum(total, n_col, n_layer):
    columns = total.shape[1]
    parts = total.reshape(n_col, n_layer, -1, columns)
    mine = lax.axis_index("layer")
    kept = lax.dynamic_index_in_dim(parts, mine, 1, keepdims=False)
    for k in range(1, n_layer):
        away = lax.dynamic_index_in_dim(parts, (mine + k) % n_layer, 1, keepdims=False)
        kept = kept + lax.ppermute(away, "layer", [(i, (i + k) % n_layer) for i in range(n_layer)])
    mine = lax.axis_index("col")
    result = lax.dynamic_index_in_dim(kept, mine, 0, keepdims=False)
    for k in range(1, n_col):
        away = lax.dynamic_index_in_dim(kept, (mine + k) % n_col, 0, keepdims=False)
        result = result + lax.ppermute(away, "col", [(i, (i + k) % n_col) for i in range(n_col)])
    return result


def local(n_row, n_col, n_layer, occupancy, tiles, panel):
    tile_rows, width = occupancy.shape
    slots, side = tiles.shape[2], tiles.shape[3]
    tiles = tiles.reshape(slots, side, side)
    panel = panel.reshape(width, side, -1)
    chunk = max(1, slots // 8)
    most = -(-slots // (2 * chunk))
    steps = (n_row - 2) * max(most, LATENCY) + most + 4
    order = ring_order(n_row)
    up = [(order[p], order[(p + 1) % n_row]) for p in range(n_row)]
    down = [(b, a) for a, b in up]
    first = [tiles[k * chunk:(k + 1) * chunk] for k in range(4) if (k + 1) * chunk <= slots]
    first = first + first[: 4 - len(first)]
    ra = lax.ppermute(first[0], "row", up)
    rb = lax.ppermute(first[1], "row", down)
    where, sched, meta = plan(occupancy, order, slots, chunk, steps)
    acc = own_product(where, meta, tiles, panel, tile_rows)
    log = blank((2, steps, chunk, side, side), tiles.dtype)

    def advance(t, sa, sb, ra, rb, acc, log):
        na = lax.ppermute(sa, "row", up)
        nb = lax.ppermute(sb, "row", down)
        acc, log, sa, sb = step(where, sched, t, ra, rb, tiles, panel, acc, log)
        return sa, sb, na, nb, acc, log

    state = advance(jnp.int32(1), first[2], first[3], ra, rb, acc, log)

    def body(carry):
        t, state = carry
        for u in range(2):
            state = advance(t + u, *state)
        return t + 2, state

    t, (_, _, ra, rb, acc, log) = lax.while_loop(lambda c: c[0] < meta[0], body, (jnp.int32(2), state))
    (acc,) = step(where, sched, t, ra, rb, tiles, panel, acc, log, relay=False)
    return scatter_sum(acc, n_col, n_layer)


def solution(mesh):
    placed = (
        P(None, ("col", "layer")),
        P(("col", "layer"), "row", None, None, None),
        P(("col", "layer"), "row"),
    )
    sizes = tuple(mesh.shape[name] for name in ("row", "col", "layer"))
    return jax.shard_map(
        functools.partial(local, *sizes), mesh=mesh, in_specs=placed, out_specs=P(("col", "layer"), "row"), check_vma=False
    )
```

time: 540 us -> 281 us (0.52)
  waiting for transfers between devices: 332 us -> 141 us
  local copies, waits for them, and re-layouts: 111 us -> 6.45 us
  Pallas kernels: 0 us -> 91.9 us
  matrix products: 58.7 us -> 0 us
  starting transfers between devices: 0.04 us -> 35.3 us
  other arithmetic: 23 us -> 2.22 us
  between operations: 13.4 us -> 0.16 us
    all_gather x1 -> x0, waiting for transfers between devices: 278 us -> none  [local(): whole = lax.all_gather(tiles, 'row', axis=1, tiled=True)]
    ppermute x0 -> x24, waiting for transfers between devices: none -> 141 us  [the longest x9 113 us: advance(): na = lax.ppermute(sa, 'row', up)]
    pallas_call x0 -> x13, Pallas kernels: none -> 91.9 us  [the longest x10 68 us: step(): pl.pallas_call(functools.partial(step_kernel, chunk, relay), out_shape=ou...]
    scatter x1 -> x0, local copies, waits for them, and re-layouts: 68.2 us -> none  [local(): dense = empty.at[target_rows, cols_at].set(flat, mode='drop')]
    dot_general x1 -> x0, matrix products: 58.7 us -> none  [local(): jnp.einsum('itab,tbn->ian', dense, panel_low, preferred_element_type=jnp....]
    reduce_scatter x1 -> x0, waiting for transfers between devices: 53.9 us -> none  [local(): lax.psum_scatter(partial_value, ('col', 'layer'), scatter_dimension=0, ti...]
    ppermute x0 -> x24, starting transfers between devices: none -> 35.3 us  [the longest x3 11.4 us: scatter_sum(): lax.ppermute(away, 'col', [(i, (i + k) % n_col) for i in range(n_col)])]
    dot_general x1 -> x0, local copies, waits for them, and re-layouts: 31.2 us -> none  [local(): jnp.einsum('itab,tbn->ian', dense, panel_low, preferred_element_type=jnp....]
  transfers between devices with their start and end apart: 2 -> 24, of which waited for: 2 -> 21; matrix products, arithmetic and copies ran while one was open for 4% -> 0% of each run, Pallas kernels for 0% -> 31%
where the time goes in v1:
time: 281 us; the launch traced here: 280 us
  waiting for transfers between devices  141 us (50%)
  Pallas kernels  91.9 us (33%)
  starting transfers between devices  35.3 us (13%)
  local copies, waits for them, and re-layouts  6.45 us (2%)
  loops' own time  2.96 us (1%)
    ppermute x9, waiting for transfers between devices, advance(): na = lax.ppermute(sa, 'row', up)  113 us
    pallas_call x10, Pallas kernels, step(): pl.pallas_call(functools.partial(step_kernel, chunk, relay), out_shape=ou...  68 us
    pallas_call x1, Pallas kernels, own_product(): pl.pallas_call(functools.partial(own_kernel, depth), out_shape=jax.ShapeD...  17.6 us
    ppermute x3, waiting for transfers between devices, scatter_sum(): lax.ppermute(away, 'col', [(i, (i + k) % n_col) for i in range(n_col)])  17.6 us
    ppermute x3, starting transfers between devices, scatter_sum(): lax.ppermute(away, 'col', [(i, (i + k) % n_col) for i in range(n_col)])  11.4 us
    ppermute x9, starting transfers between devices, advance(): na = lax.ppermute(sa, 'row', up)  10.9 us
    ppermute x9, starting transfers between devices, advance(): nb = lax.ppermute(sb, 'row', down)  9.87 us
    ppermute x9, waiting for transfers between devices, advance(): nb = lax.ppermute(sb, 'row', down)  8.41 us
  transfers between devices with their start and end apart: 24, of which 21 were waited for; matrix products, arithmetic and copies ran while one was open for 0% of the time, Pallas kernels for 31%

profile of v1, /device:TPU:0, one launch (start us, length us, event | category | flops | bytes accessed | tf_op | source)
XLA Modules:
  0.0 280.3 jit_solution(13951041418825508801)
XLA Ops:
  0.0 3.9 %slice_bitcast_fusion = (bf16[8,256,256]{2,1,0:T(8,128)(2,1)S(1)}, bf16[8,256,256]{2,1,0:T(8,128)(2,1)}, bf16[8,256,256]{2,1,0:T(8,128)(2,1)}, bf16[8,256,256]{2,1,0:T(8,128)(2,1)}) fusion(bf16[1,1,64,256,256]{4,3,2,1,0:T(8,128)(2,1)} %param.7), kind=kLoop, calls=%fused_computation.2 | loop fusion | bytes 8388608 | tf_op jit(solution)/shard_map/slice | solution.py:319
  3.9 3.0 %collective-permute-start.4 = (bf16[8,256,256]{2,1,0:T(8,128)(2,1)}, bf16[8,256,256]{2,1,0:T(8,128)(2,1)S(1)}, u32[]{:S(2)}, u32[]{:S(2)}) collective-permute-start(bf16[8,256,256]{2,1,0:T(8,128)(2,1)} %get-tuple-element.125), channel_id=1, source_target_pairs={{0,8},{8,24},{24,16},{16,0},{1,9},{9,25},{25,17},{17,1},{2,10},{10... | collective-permute-start | bytes 3145736 | tf_op jit(solution)/shard_map/ppermute | solution.py:321
  6.8 0.0 collective-permute-start.5
  6.9 2.0 collective-permute-start.6
  8.9 0.7 copy-done.2
  9.5 0.6 dynamic_slice.23.me_ref
  10.1 6.3 %plan.1 = (s32[256]{0:T(256)S(1)}, s32[16,8]{1,0:T(8,128)S(1)}, s32[4]{0:T(128)S(1)}) custom-call(s32[1]{0:T(128)} %dynamic_slice.23.me_ref, s32[4,64]{1,0:T(4,128)} %occ_ref.1), custom_call_target="tpu_custom_call" | custom-call | tf_op jit(solution)/shard_map/plan/pallas_call | solution.py:109
  16.4 17.6 %own.1.acc_in = f32[1024,512]{1,0:T(8,128)S(1)} custom-call(s32[256]{0:T(256)S(1)} %get-tuple-element.228.where_ref, s32[4]{0:T(128)S(1)} %get-tuple-element.227.meta_ref, bf16[64,256,256]{2,1,0:T(8,128)(2,1)} %bitcast.41, f32[64,256,512]{2,1,0:T(8,128)} %bitcast.38), custom_call_target="tpu_custom_call" | custom-call | flops 4294967296 | bytes 41943040 | tf_op jit(solution)/shard_map/own/pallas_call | solution.py:177
  34.0 5.9 %step.3 = (f32[1024,512]{1,0:T(8,128)S(1)}, bf16[2,16,8,256,256]{4,3,2,1,0:T(8,128)(2,1)}, bf16[8,256,256]{2,1,0:T(8,128)(2,1)}, bf16[8,256,256]{2,1,0:T(8,128)(2,1)}) custom-call(s32[256]{0:T(256)S(1)} %get-tuple-element.228.where_ref, s32[16,8]{1,0:T(8,128)S(1)} %get-tuple-element.229.sched_ref, ...), custom_call_target="tpu_custom_call", output_to_operand_aliasing={{0}: (7, {}), {1}: (8, {})} | custom-call | flops 1073741824 | bytes 12582912 | tf_op jit(solution)/shard_map/step/pallas_call | solution.py:275
  40.0 12.9 %collective-permute-done.6 = bf16[8,256,256]{2,1,0:T(8,128)(2,1)} collective-permute-done((bf16[8,256,256]{2,1,0:T(8,128)(2,1)}, bf16[8,256,256]{2,1,0:T(8,128)(2,1)}, u32[]{:S(2)}, u32[]{:S(2)}) %collective-permute-start.6) | collective-permute-done | bytes 1048608 | tf_op jit(solution)/shard_map/ppermute | solution.py:328
  52.8 1.4 collective-permute-done.7
  54.2 186.0 %while.20 = (s32[]{:T(128)}, bf16[8,256,256]{2,1,0:T(8,128)(2,1)}, bf16[8,256,256]{2,1,0:T(8,128)(2,1)}, bf16[8,256,256]{2,1,0:T(8,128)(2,1)}, bf16[8,256,256]{2...) while((s32[]{:T(128)}, bf16[8,256,256]{2,1,0:T(8,128)(2,1)}, ...), condition=%wide.region_1.0_spmd, body=%wide.region_0.0_spmd.sunk | while | flops 2147483648 | bytes 41943344 | solution.py:341
  54.8 1.6 collective-permute-start
  56.4 0.5 collective-permute-start.1
  56.9 7.6 %step.4 = (f32[1024,512]{1,0:T(8,128)}, bf16[2,16,8,256,256]{4,3,2,1,0:T(8,128)(2,1)}, bf16[8,256,256]{2,1,0:T(8,128)(2,1)}, bf16[8,256,256]{2,1,0:T(8,128)(2,1)S(1)}) custom-call(s32[256]{0:T(256)S(1)} %get-tuple-element.256.where_ref, s32[16,8]{1,0:T(8,128)S(1)} %get-tuple-element.257.sched_ref, ...), custom_call_target="tpu_custom_call", output_to_operand_aliasing={{0}: (7, {}), {1}: (8, {})} | custom-call | flops 1073741824 | bytes 12582912 | tf_op jit(solution)/shard_map/while/body/step/pallas_call | solution.py:275
  64.5 1.6 collective-permute-start.2
  66.1 0.5 collective-permute-start.3
  66.6 14.5 %collective-permute-done.ra_ref = bf16[8,256,256]{2,1,0:T(8,128)(2,1)S(1)} collective-permute-done((bf16[8,256,256]{2,1,0:T(8,128)(2,1)}, bf16[8,256,256]{2,1,0:T(8,128)(2,1)S(1)}, u32[]{:S(2)}, u32[]{:S(2)}) %collective-permute-start) | collective-permute-done | bytes 1048608 | tf_op jit(solution)/shard_map/while/body/ppermute | solution.py:328
  81.1 1.5 collective-permute-done.1.rb_ref
  82.6 7.5 %step.5 = (f32[1024,512]{1,0:T(8,128)}, bf16[2,16,8,256,256]{4,3,2,1,0:T(8,128)(2,1)}, bf16[8,256,256]{2,1,0:T(8,128)(2,1)}, bf16[8,256,256]{2,1,0:T(8,128)(2,1)}) custom-call(s32[256]{0:T(256)S(1)} %get-tuple-element.256.where_ref, s32[16,8]{1,0:T(8,128)S(1)} %get-tuple-element.257.sched_ref, ...), custom_call_target="tpu_custom_call", output_to_operand_aliasing={{0}: (7, {}), {1}: (8, {})} | custom-call | flops 1073741824 | bytes 12582912 | tf_op jit(solution)/shard_map/while/body/step/pallas_call | solution.py:275
  90.2 11.3 %collective-permute-done.2 = bf16[8,256,256]{2,1,0:T(8,128)(2,1)} collective-permute-done((bf16[8,256,256]{2,1,0:T(8,128)(2,1)}, bf16[8,256,256]{2,1,0:T(8,128)(2,1)}, u32[]{:S(2)}, u32[]{:S(2)}) %collective-permute-start.2) | collective-permute-done | bytes 1048608 | tf_op jit(solution)/shard_map/while/body/ppermute | solution.py:328
  101.4 1.2 collective-permute-done.3
  103.2 0.6 collective-permute-start
  103.9 1.5 collective-permute-start.1
  105.3 6.0 %step.4 = (f32[1024,512]{1,0:T(8,128)}, bf16[2,16,8,256,256]{4,3,2,1,0:T(8,128)(2,1)}, bf16[8,256,256]{2,1,0:T(8,128)(2,1)}, bf16[8,256,256]{2,1,0:T(8,128)(2,1)S(1)}) custom-call(s32[256]{0:T(256)S(1)} %get-tuple-element.256.where_ref, s32[16,8]{1,0:T(8,128)S(1)} %get-tuple-element.257.sched_ref, ...), custom_call_target="tpu_custom_call", output_to_operand_aliasing={{0}: (7, {}), {1}: (8, {})} | custom-call | flops 1073741824 | bytes 12582912 | tf_op jit(solution)/shard_map/while/body/step/pallas_call | solution.py:275
  111.4 2.2 collective-permute-start.2
  113.6 1.5 collective-permute-start.3
  115.1 14.4 %collective-permute-done.ra_ref = bf16[8,256,256]{2,1,0:T(8,128)(2,1)S(1)} collective-permute-done((bf16[8,256,256]{2,1,0:T(8,128)(2,1)}, bf16[8,256,256]{2,1,0:T(8,128)(2,1)S(1)}, u32[]{:S(2)}, u32[]{:S(2)}) %collective-permute-start) | collective-permute-done | bytes 1048608 | tf_op jit(solution)/shard_map/while/body/ppermute | solution.py:328
  129.5 0.6 collective-permute-done.1.rb_ref
  130.1 7.5 %step.5 = (f32[1024,512]{1,0:T(8,128)}, bf16[2,16,8,256,256]{4,3,2,1,0:T(8,128)(2,1)}, bf16[8,256,256]{2,1,0:T(8,128)(2,1)}, bf16[8,256,256]{2,1,0:T(8,128)(2,1)}) custom-call(s32[256]{0:T(256)S(1)} %get-tuple-element.256.where_ref, s32[16,8]{1,0:T(8,128)S(1)} %get-tuple-element.257.sched_ref, ...), custom_call_target="tpu_custom_call", output_to_operand_aliasing={{0}: (7, {}), {1}: (8, {})} | custom-call | flops 1073741824 | bytes 12582912 | tf_op jit(solution)/shard_map/while/body/step/pallas_call | solution.py:275
  137.6 11.1 %collective-permute-done.2 = bf16[8,256,256]{2,1,0:T(8,128)(2,1)} collective-permute-done((bf16[8,256,256]{2,1,0:T(8,128)(2,1)}, bf16[8,256,256]{2,1,0:T(8,128)(2,1)}, u32[]{:S(2)}, u32[]{:S(2)}) %collective-permute-start.2) | collective-permute-done | bytes 1048608 | tf_op jit(solution)/shard_map/while/body/ppermute | solution.py:328
  148.7 0.3 collective-permute-done.3
  149.6 0.8 collective-permute-start
  150.4 1.2 collective-permute-start.1
  151.7 7.6 %step.4 = (f32[1024,512]{1,0:T(8,128)}, bf16[2,16,8,256,256]{4,3,2,1,0:T(8,128)(2,1)}, bf16[8,256,256]{2,1,0:T(8,128)(2,1)}, bf16[8,256,256]{2,1,0:T(8,128)(2,1)S(1)}) custom-call(s32[256]{0:T(256)S(1)} %get-tuple-element.256.where_ref, s32[16,8]{1,0:T(8,128)S(1)} %get-tuple-element.257.sched_ref, ...), custom_call_target="tpu_custom_call", output_to_operand_aliasing={{0}: (7, {}), {1}: (8, {})} | custom-call | flops 1073741824 | bytes 12582912 | tf_op jit(solution)/shard_map/while/body/step/pallas_call | solution.py:275
  159.3 0.8 collective-permute-start.2
  160.2 1.7 collective-permute-start.3
  161.9 14.0 %collective-permute-done.ra_ref = bf16[8,256,256]{2,1,0:T(8,128)(2,1)S(1)} collective-permute-done((bf16[8,256,256]{2,1,0:T(8,128)(2,1)}, bf16[8,256,256]{2,1,0:T(8,128)(2,1)S(1)}, u32[]{:S(2)}, u32[]{:S(2)}) %collective-permute-start) | collective-permute-done | bytes 1048608 | tf_op jit(solution)/shard_map/while/body/ppermute | solution.py:328
  175.9 0.8 collective-permute-done.1.rb_ref
  176.7 7.5 %step.5 = (f32[1024,512]{1,0:T(8,128)}, bf16[2,16,8,256,256]{4,3,2,1,0:T(8,128)(2,1)}, bf16[8,256,256]{2,1,0:T(8,128)(2,1)}, bf16[8,256,256]{2,1,0:T(8,128)(2,1)}) custom-call(s32[256]{0:T(256)S(1)} %get-tuple-element.256.where_ref, s32[16,8]{1,0:T(8,128)S(1)} %get-tuple-element.257.sched_ref, ...), custom_call_target="tpu_custom_call", output_to_operand_aliasing={{0}: (7, {}), {1}: (8, {})} | custom-call | flops 1073741824 | bytes 12582912 | tf_op jit(solution)/shard_map/while/body/step/pallas_call | solution.py:275
  184.2 9.9 %collective-permute-done.2 = bf16[8,256,256]{2,1,0:T(8,128)(2,1)} collective-permute-done((bf16[8,256,256]{2,1,0:T(8,128)(2,1)}, bf16[8,256,256]{2,1,0:T(8,128)(2,1)}, u32[]{:S(2)}, u32[]{:S(2)}) %collective-permute-start.2) | collective-permute-done | bytes 1048608 | tf_op jit(solution)/shard_map/while/body/ppermute | solution.py:328
  194.1 1.2 collective-permute-done.3
  195.9 0.4 collective-permute-start
  196.2 1.7 collective-permute-start.1
  197.9 7.3 %step.4 = (f32[1024,512]{1,0:T(8,128)}, bf16[2,16,8,256,256]{4,3,2,1,0:T(8,128)(2,1)}, bf16[8,256,256]{2,1,0:T(8,128)(2,1)}, bf16[8,256,256]{2,1,0:T(8,128)(2,1)S(1)}) custom-call(s32[256]{0:T(256)S(1)} %get-tuple-element.256.where_ref, s32[16,8]{1,0:T(8,128)S(1)} %get-tuple-element.257.sched_ref, ...), custom_call_target="tpu_custom_call", output_to_operand_aliasing={{0}: (7, {}), {1}: (8, {})} | custom-call | flops 1073741824 | bytes 12582912 | tf_op jit(solution)/shard_map/while/body/step/pallas_call | solution.py:275
  205.3 1.0 collective-permute-start.2
  206.2 1.1 collective-permute-start.3
  207.4 14.8 %collective-permute-done.ra_ref = bf16[8,256,256]{2,1,0:T(8,128)(2,1)S(1)} collective-permute-done((bf16[8,256,256]{2,1,0:T(8,128)(2,1)}, bf16[8,256,256]{2,1,0:T(8,128)(2,1)S(1)}, u32[]{:S(2)}, u32[]{:S(2)}) %collective-permute-start) | collective-permute-done | bytes 1048608 | tf_op jit(solution)/shard_map/while/body/ppermute | solution.py:328
  222.2 0.6 collective-permute-done.1.rb_ref
  222.8 6.2 %step.5 = (f32[1024,512]{1,0:T(8,128)}, bf16[2,16,8,256,256]{4,3,2,1,0:T(8,128)(2,1)}, bf16[8,256,256]{2,1,0:T(8,128)(2,1)}, bf16[8,256,256]{2,1,0:T(8,128)(2,1)}) custom-call(s32[256]{0:T(256)S(1)} %get-tuple-element.256.where_ref, s32[16,8]{1,0:T(8,128)S(1)} %get-tuple-element.257.sched_ref, ...), custom_call_target="tpu_custom_call", output_to_operand_aliasing={{0}: (7, {}), {1}: (8, {})} | custom-call | flops 1073741824 | bytes 12582912 | tf_op jit(solution)/shard_map/while/body/step/pallas_call | solution.py:275
  229.0 9.9 %collective-permute-done.2 = bf16[8,256,256]{2,1,0:T(8,128)(2,1)} collective-permute-done((bf16[8,256,256]{2,1,0:T(8,128)(2,1)}, bf16[8,256,256]{2,1,0:T(8,128)(2,1)}, u32[]{:S(2)}, u32[]{:S(2)}) %collective-permute-start.2) | collective-permute-done | bytes 1048608 | tf_op jit(solution)/shard_map/while/body/ppermute | solution.py:328
  238.9 0.8 collective-permute-done.3
  240.2 4.7 %last.1 = f32[1024,512]{1,0:T(8,128)} custom-call(s32[256]{0:T(256)S(1)} %get-tuple-element.279, s32[16,8]{1,0:T(8,128)S(1)} %get-tuple-element.269, s32[1]{0:T(128)} %bitcast.9.t_ref, bf16[8,256,256]{2,1,0:T(8,128)(2,1)} %get-tuple-element.95.ra_ref, bf16[8,256,256]{2,1,0:T(8,128)(2,1)} %get-tuple-element.96.rb_ref, ...), custom_call_target="tpu_custom_call", output_to_operand_aliasing={{}: (7, {})} | custom-call | flops 1073741824 | bytes 12582912 | tf_op jit(solution)/shard_map/last/pallas_call | solution.py:275
  245.0 1.3 dynamic-slice_bitcast_fusion
  246.3 0.1 collective-permute-start.8
  246.4 2.6 collective-permute-done.8
  249.0 1.4 bitcast_add_fusion
  250.5 0.1 dynamic-slice_bitcast_fusion.3
  250.5 2.2 collective-permute-start.10
  252.7 8.7 %collective-permute-start.11 = (f32[128,512]{1,0:T(8,128)S(1)}, f32[128,512]{1,0:T(8,128)S(1)}, u32[]{:S(2)}, u32[]{:S(2)}) collective-permute-start(f32[128,512]{1,0:T(8,128)S(1)} %get-tuple-element.128), channel_id=1, source_target_pairs={{0,6},{2,0},{4,2},{6,4},{1,7},{3,1},{5,3},{7,5},{8,14},{10,8},{12,... | collective-permute-start | bytes 786440 | tf_op jit(solution)/shard_map/ppermute | solution.py:304
  261.5 0.5 collective-permute-start.9
  262.0 6.6 %collective-permute-done.11 = f32[128,512]{1,0:T(8,128)S(1)} collective-permute-done((f32[128,512]{1,0:T(8,128)S(1)}, f32[128,512]{1,0:T(8,128)S(1)}, u32[]{:S(2)}, u32[]{:S(2)}) %collective-permute-start.11) | collective-permute-done | bytes 262176 | tf_op jit(solution)/shard_map/ppermute | solution.py:304
  268.5 11.0 %collective-permute-done.9 = f32[128,512]{1,0:T(8,128)S(1)} collective-permute-done((f32[128,512]{1,0:T(8,128)S(1)}, f32[128,512]{1,0:T(8,128)S(1)}, u32[]{:S(2)}, u32[]{:S(2)}) %collective-permute-start.9) | collective-permute-done | bytes 262176 | tf_op jit(solution)/shard_map/ppermute | solution.py:304
  279.5 0.8 fusion.1
  (10 shorter events, 0.0 us)
Async XLA Ops:
  3.9 30.1 %collective-permute-start.4 = (bf16[8,256,256]{2,1,0:T(8,128)(2,1)}, bf16[8,256,256]{2,1,0:T(8,128)(2,1)S(1)}, u32[]{:S(2)}, u32[]{:S(2)}) collective-permute-start(bf16[8,256,256]{2,1,0:T(8,128)(2,1)} %get-tuple-element.125), channel_id=1, source_target_pairs={{0,8},{8,24},{24,16},{16,0},{1,9},{9,25},{25,17},{17,1},{2,10},{10... | collective-permute-start | bytes 3145736 | tf_op jit(solution)/shard_map/ppermute | solution.py:321
  6.8 27.2 %collective-permute-start.5 = (bf16[8,256,256]{2,1,0:T(8,128)(2,1)}, bf16[8,256,256]{2,1,0:T(8,128)(2,1)S(1)}, u32[]{:S(2)}, u32[]{:S(2)}) collective-permute-start(bf16[8,256,256]{2,1,0:T(8,128)(2,1)} %get-tuple-element.124), channel_id=1, source_target_pairs={{8,0},{24,8},{16,24},{0,16},{9,1},{25,9},{17,25},{1,17},{10,2},{26... | collective-permute-start | bytes 3145736 | tf_op jit(solution)/shard_map/ppermute | solution.py:322
  6.9 45.9 %collective-permute-start.6 = (bf16[8,256,256]{2,1,0:T(8,128)(2,1)}, bf16[8,256,256]{2,1,0:T(8,128)(2,1)}, u32[]{:S(2)}, u32[]{:S(2)}) collective-permute-start(bf16[8,256,256]{2,1,0:T(8,128)(2,1)} %get-tuple-element.126), channel_id=1, source_target_pairs={{0,8},{8,24},{24,16},{16,0},{1,9},{9,25},{25,17},{17,1},{2,10},{10... | collective-permute-start | bytes 3145736 | tf_op jit(solution)/shard_map/ppermute | solution.py:328
  8.9 45.4 %collective-permute-start.7 = (bf16[8,256,256]{2,1,0:T(8,128)(2,1)S(1)}, bf16[8,256,256]{2,1,0:T(8,128)(2,1)}, u32[]{:S(2)}, u32[]{:S(2)}) collective-permute-start(bf16[8,256,256]{2,1,0:T(8,128)(2,1)S(1)} %get-tuple-element.123), channel_id=1, source_target_pairs={{8,0},{24,8},{16,24},{0,16},{9,1},{25,9},{17,25},{1,17},{10,2},{26... | collective-permute-start | bytes 3145736 | tf_op jit(solution)/shard_map/ppermute | solution.py:329
  8.9 0.7 copy-start.2
  16.4 17.6 %copy-start.1 = (s32[4]{0:T(128)}, s32[4]{0:T(128)S(1)}, u32[]{:S(2)}) copy-start(s32[4]{0:T(128)S(1)} %get-tuple-element.227.meta_ref) | copy-start | bytes 52
  39.9 14.3 %copy-start = (f32[1024,512]{1,0:T(8,128)}, f32[1024,512]{1,0:T(8,128)S(1)}, u32[]{:S(2)}) copy-start(f32[1024,512]{1,0:T(8,128)S(1)} %get-tuple-element.225) | copy-start | bytes 6291460
  54.8 26.3 %collective-permute-start = (bf16[8,256,256]{2,1,0:T(8,128)(2,1)}, bf16[8,256,256]{2,1,0:T(8,128)(2,1)S(1)}, u32[]{:S(2)}, u32[]{:S(2)}) collective-permute-start(bf16[8,256,256]{2,1,0:T(8,128)(2,1)} %get-tuple-element.235), channel_id=1, source_target_pairs={{0,8},{8,24},{24,16},{16,0},{1,9},{9,25},{25,17},{17,1},{2,10},{10... | collective-permute-start | bytes 3145736 | tf_op jit(solution)/shard_map/while/body/ppermute | solution.py:328
  56.4 26.2 %collective-permute-start.1 = (bf16[8,256,256]{2,1,0:T(8,128)(2,1)}, bf16[8,256,256]{2,1,0:T(8,128)(2,1)S(1)}, u32[]{:S(2)}, u32[]{:S(2)}) collective-permute-start(bf16[8,256,256]{2,1,0:T(8,128)(2,1)} %get-tuple-element.236), channel_id=1, source_target_pairs={{8,0},{24,8},{16,24},{0,16},{9,1},{25,9},{17,25},{1,17},{10,2},{26... | collective-permute-start | bytes 3145736 | tf_op jit(solution)/shard_map/while/body/ppermute | solution.py:329
  64.5 36.9 %collective-permute-start.2 = (bf16[8,256,256]{2,1,0:T(8,128)(2,1)}, bf16[8,256,256]{2,1,0:T(8,128)(2,1)}, u32[]{:S(2)}, u32[]{:S(2)}) collective-permute-start(bf16[8,256,256]{2,1,0:T(8,128)(2,1)} %get-tuple-element.216), channel_id=1, source_target_pairs={{0,8},{8,24},{24,16},{16,0},{1,9},{9,25},{25,17},{17,1},{2,10},{10... | collective-permute-start | bytes 3145736 | tf_op jit(solution)/shard_map/while/body/ppermute | solution.py:328
  66.1 36.6 %collective-permute-start.3 = (bf16[8,256,256]{2,1,0:T(8,128)(2,1)S(1)}, bf16[8,256,256]{2,1,0:T(8,128)(2,1)}, u32[]{:S(2)}, u32[]{:S(2)}) collective-permute-start(bf16[8,256,256]{2,1,0:T(8,128)(2,1)S(1)} %get-tuple-element.217), channel_id=1, source_target_pairs={{8,0},{24,8},{16,24},{0,16},{9,1},{25,9},{17,25},{1,17},{10,2},{26... | collective-permute-start | bytes 3145736 | tf_op jit(solution)/shard_map/while/body/ppermute | solution.py:329
  103.2 26.3 %collective-permute-start = (bf16[8,256,256]{2,1,0:T(8,128)(2,1)}, bf16[8,256,256]{2,1,0:T(8,128)(2,1)S(1)}, u32[]{:S(2)}, u32[]{:S(2)}) collective-permute-start(bf16[8,256,256]{2,1,0:T(8,128)(2,1)} %get-tuple-element.235), channel_id=1, source_target_pairs={{0,8},{8,24},{24,16},{16,0},{1,9},{9,25},{25,17},{17,1},{2,10},{10... | collective-permute-start | bytes 3145736 | tf_op jit(solution)/shard_map/while/body/ppermute | solution.py:328
  103.9 26.2 %collective-permute-start.1 = (bf16[8,256,256]{2,1,0:T(8,128)(2,1)}, bf16[8,256,256]{2,1,0:T(8,128)(2,1)S(1)}, u32[]{:S(2)}, u32[]{:S(2)}) collective-permute-start(bf16[8,256,256]{2,1,0:T(8,128)(2,1)} %get-tuple-element.236), channel_id=1, source_target_pairs={{8,0},{24,8},{16,24},{0,16},{9,1},{25,9},{17,25},{1,17},{10,2},{26... | collective-permute-start | bytes 3145736 | tf_op jit(solution)/shard_map/while/body/ppermute | solution.py:329
  111.4 37.3 %collective-permute-start.2 = (bf16[8,256,256]{2,1,0:T(8,128)(2,1)}, bf16[8,256,256]{2,1,0:T(8,128)(2,1)}, u32[]{:S(2)}, u32[]{:S(2)}) collective-permute-start(bf16[8,256,256]{2,1,0:T(8,128)(2,1)} %get-tuple-element.216), channel_id=1, source_target_pairs={{0,8},{8,24},{24,16},{16,0},{1,9},{9,25},{25,17},{17,1},{2,10},{10... | collective-permute-start | bytes 3145736 | tf_op jit(solution)/shard_map/while/body/ppermute | solution.py:328
  113.6 35.4 %collective-permute-start.3 = (bf16[8,256,256]{2,1,0:T(8,128)(2,1)S(1)}, bf16[8,256,256]{2,1,0:T(8,128)(2,1)}, u32[]{:S(2)}, u32[]{:S(2)}) collective-permute-start(bf16[8,256,256]{2,1,0:T(8,128)(2,1)S(1)} %get-tuple-element.217), channel_id=1, source_target_pairs={{8,0},{24,8},{16,24},{0,16},{9,1},{25,9},{17,25},{1,17},{10,2},{26... | collective-permute-start | bytes 3145736 | tf_op jit(solution)/shard_map/while/body/ppermute | solution.py:329
  149.6 26.3 %collective-permute-start = (bf16[8,256,256]{2,1,0:T(8,128)(2,1)}, bf16[8,256,256]{2,1,0:T(8,128)(2,1)S(1)}, u32[]{:S(2)}, u32[]{:S(2)}) collective-permute-start(bf16[8,256,256]{2,1,0:T(8,128)(2,1)} %get-tuple-element.235), channel_id=1, source_target_pairs={{0,8},{8,24},{24,16},{16,0},{1,9},{9,25},{25,17},{17,1},{2,10},{10... | collective-permute-start | bytes 3145736 | tf_op jit(solution)/shard_map/while/body/ppermute | solution.py:328
  150.4 26.2 %collective-permute-start.1 = (bf16[8,256,256]{2,1,0:T(8,128)(2,1)}, bf16[8,256,256]{2,1,0:T(8,128)(2,1)S(1)}, u32[]{:S(2)}, u32[]{:S(2)}) collective-permute-start(bf16[8,256,256]{2,1,0:T(8,128)(2,1)} %get-tuple-element.236), channel_id=1, source_target_pairs={{8,0},{24,8},{16,24},{0,16},{9,1},{25,9},{17,25},{1,17},{10,2},{26... | collective-permute-start | bytes 3145736 | tf_op jit(solution)/shard_map/while/body/ppermute | solution.py:329
  159.3 34.8 %collective-permute-start.2 = (bf16[8,256,256]{2,1,0:T(8,128)(2,1)}, bf16[8,256,256]{2,1,0:T(8,128)(2,1)}, u32[]{:S(2)}, u32[]{:S(2)}) collective-permute-start(bf16[8,256,256]{2,1,0:T(8,128)(2,1)} %get-tuple-element.216), channel_id=1, source_target_pairs={{0,8},{8,24},{24,16},{16,0},{1,9},{9,25},{25,17},{17,1},{2,10},{10... | collective-permute-start | bytes 3145736 | tf_op jit(solution)/shard_map/while/body/ppermute | solution.py:328
  160.2 35.1 %collective-permute-start.3 = (bf16[8,256,256]{2,1,0:T(8,128)(2,1)S(1)}, bf16[8,256,256]{2,1,0:T(8,128)(2,1)}, u32[]{:S(2)}, u32[]{:S(2)}) collective-permute-start(bf16[8,256,256]{2,1,0:T(8,128)(2,1)S(1)} %get-tuple-element.217), channel_id=1, source_target_pairs={{8,0},{24,8},{16,24},{0,16},{9,1},{25,9},{17,25},{1,17},{10,2},{26... | collective-permute-start | bytes 3145736 | tf_op jit(solution)/shard_map/while/body/ppermute | solution.py:329
  195.9 26.3 %collective-permute-start = (bf16[8,256,256]{2,1,0:T(8,128)(2,1)}, bf16[8,256,256]{2,1,0:T(8,128)(2,1)S(1)}, u32[]{:S(2)}, u32[]{:S(2)}) collective-permute-start(bf16[8,256,256]{2,1,0:T(8,128)(2,1)} %get-tuple-element.235), channel_id=1, source_target_pairs={{0,8},{8,24},{24,16},{16,0},{1,9},{9,25},{25,17},{17,1},{2,10},{10... | collective-permute-start | bytes 3145736 | tf_op jit(solution)/shard_map/while/body/ppermute | solution.py:328
  196.2 26.5 %collective-permute-start.1 = (bf16[8,256,256]{2,1,0:T(8,128)(2,1)}, bf16[8,256,256]{2,1,0:T(8,128)(2,1)S(1)}, u32[]{:S(2)}, u32[]{:S(2)}) collective-permute-start(bf16[8,256,256]{2,1,0:T(8,128)(2,1)} %get-tuple-element.236), channel_id=1, source_target_pairs={{8,0},{24,8},{16,24},{0,16},{9,1},{25,9},{17,25},{1,17},{10,2},{26... | collective-permute-start | bytes 3145736 | tf_op jit(solution)/shard_map/while/body/ppermute | solution.py:329
  205.3 33.6 %collective-permute-start.2 = (bf16[8,256,256]{2,1,0:T(8,128)(2,1)}, bf16[8,256,256]{2,1,0:T(8,128)(2,1)}, u32[]{:S(2)}, u32[]{:S(2)}) collective-permute-start(bf16[8,256,256]{2,1,0:T(8,128)(2,1)} %get-tuple-element.216), channel_id=1, source_target_pairs={{0,8},{8,24},{24,16},{16,0},{1,9},{9,25},{25,17},{17,1},{2,10},{10... | collective-permute-start | bytes 3145736 | tf_op jit(solution)/shard_map/while/body/ppermute | solution.py:328
  206.2 33.4 %collective-permute-start.3 = (bf16[8,256,256]{2,1,0:T(8,128)(2,1)S(1)}, bf16[8,256,256]{2,1,0:T(8,128)(2,1)}, u32[]{:S(2)}, u32[]{:S(2)}) collective-permute-start(bf16[8,256,256]{2,1,0:T(8,128)(2,1)S(1)} %get-tuple-element.217), channel_id=1, source_target_pairs={{8,0},{24,8},{16,24},{0,16},{9,1},{25,9},{17,25},{1,17},{10,2},{26... | collective-permute-start | bytes 3145736 | tf_op jit(solution)/shard_map/while/body/ppermute | solution.py:329
  246.3 2.7 collective-permute-start.8
  250.5 11.4 %collective-permute-start.10 = (f32[128,512]{1,0:T(8,128)S(1)}, f32[128,512]{1,0:T(8,128)S(1)}, u32[]{:S(2)}, u32[]{:S(2)}) collective-permute-start(f32[128,512]{1,0:T(8,128)S(1)} %get-tuple-element.129), channel_id=1, source_target_pairs={{0,4},{2,6},{4,0},{6,2},{1,5},{3,7},{5,1},{7,3},{8,12},{10,14},{12... | collective-permute-start | bytes 786440 | tf_op jit(solution)/shard_map/ppermute | solution.py:304
  252.7 15.8 %collective-permute-start.11 = (f32[128,512]{1,0:T(8,128)S(1)}, f32[128,512]{1,0:T(8,128)S(1)}, u32[]{:S(2)}, u32[]{:S(2)}) collective-permute-start(f32[128,512]{1,0:T(8,128)S(1)} %get-tuple-element.128), channel_id=1, source_target_pairs={{0,6},{2,0},{4,2},{6,4},{1,7},{3,1},{5,3},{7,5},{8,14},{10,8},{12,... | collective-permute-start | bytes 786440 | tf_op jit(solution)/shard_map/ppermute | solution.py:304
  261.5 18.1 %collective-permute-start.9 = (f32[128,512]{1,0:T(8,128)S(1)}, f32[128,512]{1,0:T(8,128)S(1)}, u32[]{:S(2)}, u32[]{:S(2)}) collective-permute-start(f32[128,512]{1,0:T(8,128)S(1)} %get-tuple-element.127), channel_id=1, source_target_pairs={{0,2},{2,4},{4,6},{6,0},{1,3},{3,5},{5,7},{7,1},{8,10},{10,12},{12... | collective-permute-start | bytes 786440 | tf_op jit(solution)/shard_map/ppermute | solution.py:304
